TPU v7x, 32 devices: a whole 2x2x4 slice. The times are simulated.
32 devices in a mesh: seq: 8 (over y, x, core), tp: 4 (over z).
Axes of the slice: x: 2, y: 2, z: 4, core: 2. Of those that a mesh axis runs over, the one named last changes fastest.
Arguments:
- projected: bfloat16 [1, 8192, 3, 4096], P(None, 'seq', None, 'tp'), may hold values from -6 to 6
- short_kernel: float32 [3, 3, 4096], P(None, None, 'tp'), may hold values from -3 to 3
- filters: float32 [2, 4096, 8192], P(None, ('tp', 'seq')), may hold values from -2 to 2
- skip_gain: float32 [2, 4096], P(None, ('tp', 'seq')), may hold values from -3 to 3
- out_weight: bfloat16 [4096, 4096], P('tp'), may hold values from -0.09375 to 0.09375
- out_grad: bfloat16 [1, 8192, 4096], P(None, 'seq', 'tp'), may hold values from -6 to 6
Outputs:
- output: bfloat16 [1, 8192, 4096], P(None, 'seq', 'tp')
- projected_grad: bfloat16 [1, 8192, 3, 4096], P(None, 'seq', None, 'tp')
- filter_grad: float32 [2, 4096, 8192], P(None, ('tp', 'seq'))
All inputs are finite; a program needn't handle non-finite values.
Results may differ from a plain program's by a relative error of at most 0.0095.
Values may be sent and summed in bfloat16 or wider, within the bound.
A program may use at most 384 MiB of HBM per device.

v0:
```python
import math
import jax
import jax.numpy as jnp
from jax import lax
from jax.sharding import PartitionSpec as P

LEN = 8192
SEQS = 1
precise = lax.Precision.HIGH


def from_behind(block, axis, distance):
    devices = range(lax.axis_size(axis))
    route = [(i - distance, i) for i in devices if i - distance in devices]
    return lax.ppermute(block, axis, route)


def dft_tables(length):
    total = 2 * length
    levels = total.bit_length() - 1
    outer = 2 ** (levels // 2)
    inner = total // outer
    halfway = outer // 2
    outer_ids = jnp.arange(outer, dtype=jnp.int32)
    inner_ids = jnp.arange(inner, dtype=jnp.int32)
    outer_angle = (outer_ids[:, None] * outer_ids[None, :] % outer).astype(jnp.float32) * (
        2.0 * math.pi / outer
    )
    outer_cos = jnp.cos(outer_angle)
    outer_sin = jnp.sin(outer_angle)
    opening = jnp.concatenate([outer_cos[:, :halfway], -outer_sin[:, :halfway]], axis=0)
    closing = jnp.concatenate([outer_cos[:halfway, :], -outer_sin[:halfway, :]], axis=1) / total
    inner_angle = (inner_ids[:, None] * inner_ids[None, :] % inner).astype(jnp.float32) * (
        2.0 * math.pi / inner
    )
    inner_cos = jnp.cos(inner_angle)
    inner_sin = jnp.sin(inner_angle)
    forward_mix = jnp.concatenate(
        [
            jnp.concatenate([inner_cos, -inner_sin], axis=1),
            jnp.concatenate([inner_sin, inner_cos], axis=1),
        ],
        axis=0,
    )
    inverse_mix = jnp.concatenate(
        [
            jnp.concatenate([inner_cos, inner_sin], axis=1),
            jnp.concatenate([-inner_sin, inner_cos], axis=1),
        ],
        axis=0,
    )
    twist_angle = (outer_ids[:, None] * inner_ids[None, :] % total).astype(jnp.float32) * (
        2.0 * math.pi / total
    )
    return (opening, closing, forward_mix, inverse_mix, jnp.cos(twist_angle), -jnp.sin(twist_angle))


def forward_dft(signal, tables):
    opening, closing, forward_mix, inverse_mix, twist_real, twist_imag = tables
    outer, inner = twist_real.shape
    row_count = signal.shape[0]
    shaped = signal.reshape(row_count, outer // 2, inner)
    mixed = jnp.einsum("kn,rnm->rkm", opening, shaped, precision=precise)
    real_part = mixed[:, :outer]
    imag_part = mixed[:, outer:]
    turned = jnp.concatenate(
        [
            real_part * twist_real - imag_part * twist_imag,
            real_part * twist_imag + imag_part * twist_real,
        ],
        axis=2,
    )
    spectrum = jnp.dot(turned.reshape(row_count * outer, 2 * inner), forward_mix, precision=precise)
    return spectrum.reshape(row_count, outer, 2 * inner)


def inverse_dft(spectrum, tables):
    opening, closing, forward_mix, inverse_mix, twist_real, twist_imag = tables
    outer, inner = twist_real.shape
    row_count = spectrum.shape[0]
    reverted = jnp.dot(
        spectrum.reshape(row_count * outer, 2 * inner), inverse_mix, precision=precise
    )
    reverted = reverted.reshape(row_count, outer, 2 * inner)
    real_part = reverted[..., :inner]
    imag_part = reverted[..., inner:]
    turned = jnp.concatenate(
        [
            real_part * twist_real + imag_part * twist_imag,
            imag_part * twist_real - real_part * twist_imag,
        ],
        axis=1,
    )
    signal = jnp.einsum("nk,rkm->rnm", closing, turned, precision=precise)
    return signal.reshape(row_count, -1)


def forward_rows(signal, tables):
    lead = signal.shape[:-1]
    flat_spec = forward_dft(signal.reshape(-1, signal.shape[-1]), tables)
    return flat_spec.reshape(lead + flat_spec.shape[1:])


def inverse_rows(spectrum, tables):
    lead = spectrum.shape[:-2]
    flat_signal = inverse_dft(spectrum.reshape((-1,) + spectrum.shape[-2:]), tables)
    return flat_signal.reshape(lead + (flat_signal.shape[-1],))


def spectral_product(left, right, conjugate):
    inner = left.shape[-1] // 2
    left_real = left[..., :inner]
    left_imag = -left[..., inner:] if conjugate else left[..., inner:]
    right_real = right[..., :inner]
    right_imag = right[..., inner:]
    return jnp.concatenate(
        [
            left_real * right_real - left_imag * right_imag,
            left_real * right_imag + left_imag * right_real,
        ],
        axis=-1,
    )


def edge_frames(block, shift_by):
    return from_behind(block, "seq", shift_by)


def to_channels(block):
    moved = lax.all_to_all(block, "seq", split_axis=3, concat_axis=2, tiled=True)
    return jnp.swapaxes(moved, 2, 3)


def to_frames(block):
    return lax.all_to_all(jnp.swapaxes(block, 2, 3), "seq", split_axis=2, concat_axis=3, tiled=True)


def local(projected, short_kernel, filters, skip_gain, out_weight, out_grad):
    seq_count, frames, _, local_width = projected.shape
    tables = dft_tables(LEN)
    edge_rows = edge_frames(projected[:, frames - 2 :], 1)
    padded = jnp.concatenate([edge_rows, projected], axis=1).astype(jnp.float32)
    short = sum(
        (
            short_kernel[:, offset, :] * padded[:, 2 - offset : 2 - offset + frames]
            for offset in range(3)
        )
    ).astype(jnp.bfloat16)
    outgoing = jnp.transpose(short, (2, 0, 1, 3))
    channel = to_channels(outgoing)
    short_v = channel[0].astype(jnp.float32)
    short_x1 = channel[1].astype(jnp.float32)
    gain_zero = skip_gain[0][None, :, None]
    gain_one = skip_gain[1][None, :, None]
    spec_zero = forward_rows(filters[0], tables)[None]
    spec_one = forward_rows(filters[1], tables)[None]
    spec_short = forward_rows(short_v, tables)
    first_conv = gain_zero * short_v + inverse_rows(
        spectral_product(spec_short, spec_zero, False), tables
    )
    middle = short_x1 * first_conv
    spec_middle = forward_rows(middle, tables)
    second = (
        gain_one * middle + inverse_rows(spectral_product(spec_middle, spec_one, False), tables)
    ).astype(jnp.bfloat16)
    short_x2 = channel[2].astype(jnp.float32)
    returned = (short_x2 * second.astype(jnp.float32)).astype(jnp.bfloat16)
    arrived = to_frames(returned[None])[0]
    flat_gated = arrived.reshape(seq_count * frames, local_width)
    summed = lax.psum_scatter(
        lax.dot_general(
            out_weight, flat_gated, (((0,), (1,)), ((), ())), preferred_element_type=jnp.float32
        ).astype(jnp.bfloat16),
        "tp",
        scatter_dimension=0,
        tiled=True,
    ).astype(jnp.float32)
    output = jnp.transpose(summed).reshape(seq_count, frames, local_width).astype(jnp.bfloat16)
    back_gated = lax.dot_general(
        lax.all_gather(out_grad, "tp", axis=2, tiled=True),
        out_weight,
        (((2,), (1,)), ((), ())),
        preferred_element_type=jnp.float32,
    ).astype(jnp.bfloat16)
    received = to_channels(back_gated[None])[0]
    back_gated_chan = received.astype(jnp.float32)
    back_second = (back_gated_chan * short_x2).astype(jnp.bfloat16).astype(jnp.float32)
    back_x2 = (back_gated_chan * second.astype(jnp.float32)).astype(jnp.bfloat16)
    spec_back_sec = forward_rows(back_second, tables)
    back_middle = gain_one * back_second + inverse_rows(
        spectral_product(spec_one, spec_back_sec, True), tables
    )
    grad_one = inverse_rows(
        jnp.sum(spectral_product(spec_middle, spec_back_sec, True), axis=0), tables
    )
    back_x1 = (back_middle * first_conv).astype(jnp.bfloat16)
    back_first = back_middle * short_x1
    spec_back_first = forward_rows(back_first, tables)
    back_v = (
        gain_zero * back_first
        + inverse_rows(spectral_product(spec_zero, spec_back_first, True), tables)
    ).astype(jnp.bfloat16)
    grad_zero = inverse_rows(
        jnp.sum(spectral_product(spec_short, spec_back_first, True), axis=0), tables
    )
    filter_grad = jnp.stack([grad_zero, grad_one]) * (SEQS * LEN) ** (-0.5)
    grads_chan = jnp.stack([back_v, back_x1, back_x2])
    grads_frames = jnp.transpose(to_frames(grads_chan), (1, 2, 0, 3))
    next_rows = edge_frames(grads_frames[:, :2], -1)
    tail = jnp.concatenate([grads_frames, next_rows], axis=1).astype(jnp.float32)
    projected_grad = sum(
        (short_kernel[:, offset, :] * tail[:, offset : offset + frames] for offset in range(3))
    ).astype(jnp.bfloat16)
    return (output, projected_grad, filter_grad)


def solution(mesh):
    in_specs = (
        P(None, "seq", None, "tp"),
        P(None, None, "tp"),
        P(None, ("tp", "seq"), None),
        P(None, ("tp", "seq")),
        P("tp", None),
        P(None, "seq", "tp"),
    )
    out_specs = (P(None, "seq", "tp"), P(None, "seq", None, "tp"), P(None, ("tp", "seq"), None))
    return jax.shard_map(local, mesh=mesh, in_specs=in_specs, out_specs=out_specs, check_vma=False)
```

profile of v0, /device:TPU:1, one launch (start us, length us, event | category | flops | bytes accessed | tf_op | source)
XLA Modules:
  0.0 1164.1 jit_solution(14599692841856185292)
XLA Ops:
  14.2 8.9 copy.400
  23.5 11.4 maximum_convert_fusion
  35.0 21.4 %fusion.92 = bf16[3,1,1024,1024]{2,3,0,1:T(8,128)(2,1)} fusion(f32[1,1026,3,1024]{1,3,2,0:T(8,128)} %maximum_convert_fusion, f32[3,1024]{1,0:T(4,128)S(1)} %get-tuple-element.85, f32[3,1024]{1,0:T(4,128)S(1)} %get-tuple-element.86, f32[3,1024]{1,0:T(4,128)S(1)} %bitcast.207), kind=kLoop, calls=%fused_computation.138 | loop fusion | flops 18874368 | bytes 44077056 | tf_op jit(solution)/shard_map/transpose | solution.py:149
  56.3 11.6 copy.401
  81.1 9.7 convolution_bitcast_fusion.2
  90.8 9.7 convolution_bitcast_fusion.4
  100.5 61.5 %all-to-all-done = bf16[3,1,1024,1024]{2,0,1,3:T(4,128)(2,1)} async-done(((bf16[3,1,1024,1024]{2,0,1,3:T(4,128)(2,1)}), bf16[3,1,1024,1024]{2,0,1,3:T(4,128)(2,1)}, u32[]{:S(2)}, u32[]{:S(2)}) %all-to-all-start) | async-done | bytes 6291488 | tf_op jit(solution)/shard_map/all_to_all | solution.py:130
  162.0 8.6 copy.402
  179.2 13.9 %convert_bitcast_fusion.1 = bf16[1,1,1024,1024]{3,2,1,0:T(8,128)(2,1)S(1)} fusion(bf16[1024,4096]{1,0:T(8,128)(2,1)} %param.10, bf16[1,1024,4096]{2,1,0:T(8,128)(2,1)} %all-gather.2.cloned.1.call-done), kind=kOutput, calls=%fused_computation.170 | convolution fusion | flops 8590983168 | bytes 18874368 | tf_op jit(solution)/shard_map/dot_general | solution.py:179
  201.2 12.7 %reduce = bf16[1024,1024]{1,0:T(8,128)(2,1)S(1)} reduce(bf16[1024,1,1,1024]{3,2,1,0:T(2,128)(2,1)} %bitcast.199, bf16[]{:T(256)} %broadcast.130), dimensions={1,2}, to_apply=%bitcast.163.reduce_sub_computation | reduce | bytes 4194306
  255.0 11.1 copy.427
  282.1 25.6 %multiply_subtract_fusion.9 = (f32[128,128,128]{1,2,0:T(8,128)}, f32[128,128,128]{1,2,0:T(8,128)}, f32[128,128,128]{1,2,0:T(8,128)}, f32[128,128,128]{1,2,0:T(8,128)}) fusion(f32[128,256,128]{1,2,0:T(8,128)} %convolution_bitcast_fusion.1, f32[128,128]{0,1:T(8,128)S(1)} %copy.407, f32[128,128]{0,1:T(8,128)S(1)} %copy.406, ...), kind=kLoop, calls=%fused_computation.118 | loop fusion | flops 25165824 | bytes 67239936 | tf_op jit(solution)/shard_map/sub | solution.py:68
  307.8 20.6 %fusion.75 = f32[1,128,128,256]{3,2,1,0:T(8,128)} fusion(f32[128,128,128]{1,2,0:T(8,128)} %get-tuple-element.43, f32[128,128,128]{1,2,0:T(8,128)} %get-tuple-element.42, f32[128,128]{1,0:T(8,128)S(1)} %get-tuple-element.88, f32[128,128]{1,0:T(8,128)S(1)} %get-tuple-element.87, f32[128,128]{1,0:T(8,128)S(1)} %fusion.158), kind=kOutput, calls=%fused_computation.85 | convolution fusion | flops 6446841856 | bytes 33751040 | tf_op jit(solution)/shard_map/dot_general | solution.py:73
  328.4 20.3 %fusion.78 = f32[1,128,128,256]{3,2,1,0:T(8,128)} fusion(f32[128,128,128]{1,2,0:T(8,128)} %get-tuple-element.78, f32[128,128,128]{1,2,0:T(8,128)} %get-tuple-element.79, f32[128,128]{1,0:T(8,128)S(1)} %get-tuple-element.88, f32[128,128]{1,0:T(8,128)S(1)} %get-tuple-element.87, f32[128,128]{1,0:T(8,128)S(1)} %fusion.158), kind=kOutput, calls=%fused_computation.86 | convolution fusion | flops 6446841856 | bytes 33751040 | tf_op jit(solution)/shard_map/dot_general | solution.py:73
  348.6 18.9 %multiply_subtract_fusion.8 = (f32[1,128,128,128]{3,2,1,0:T(8,128)}, f32[1,128,128,128]{3,2,1,0:T(8,128)}) fusion(f32[1,128,128,256]{3,2,1,0:T(8,128)} %fusion.75, f32[1,128,128,256]{3,2,1,0:T(8,128)} %fusion.78), kind=kLoop, calls=%fused_computation.116 | loop fusion | flops 14680064 | bytes 50331648 | tf_op jit(solution)/shard_map/sub | solution.py:118
  367.5 14.0 %fusion.34 = f32[128,128,256]{1,2,0:T(8,128)} fusion(f32[1,128,128,128]{3,2,1,0:T(8,128)} %get-tuple-element.27, f32[1,128,128,128]{3,2,1,0:T(8,128)} %get-tuple-element.26, f32[128,128]{1,0:T(8,128)S(1)} %get-tuple-element.88, f32[128,128]{1,0:T(8,128)S(1)} %fusion.158, f32[128,128]{1,0:T(8,128)S(1)} %get-tuple-element.87), kind=kOutput, calls=%fused_computation.37 | convolution fusion | flops 6446841856 | bytes 33751040 | tf_op jit(solution)/shard_map/dot_general | solution.py:81
  388.7 9.2 fusion.113
  403.3 14.3 %convolution_bitcast_fusion = f32[128,256,128]{1,2,0:T(8,128)} fusion(f32[128,64,128]{2,1,0:T(8,128)} %copy.481, f32[128,64,128]{2,1,0:T(8,128)} %fusion.113, bf16[128,64,128]{2,1,0:T(8,128)(2,1)S(1)} %copy.485, f32[128]{0:T(128)S(1)} %copy-done.17, f32[128,64]{1,0:T(8,128)S(1)} %slice_negate_fusion, f32[128,64]{1,0:T(8,128)S(1)} %bitcast.192), kind=kOutput, calls=%fused_computation.90 | convolution fusion | flops 1614823424 | bytes 27329024 | tf_op jit(solution)/shard_map/kn,rnm->rkm/dot_general | solution.py:63
  417.7 32.0 %multiply_subtract_fusion.6 = (f32[128,128,128]{1,2,0:T(8,128)}, f32[128,128,128]{1,2,0:T(8,128)}, f32[128,128,128]{1,2,0:T(8,128)}, f32[128,128,128]{1,2,0:T(8,...) fusion(f32[128,256,128]{1,2,0:T(8,128)} %convolution_bitcast_fusion, f32[128,128]{0,1:T(8,128)S(1)} %copy.407, ...), kind=kLoop, calls=%fused_computation.112 | loop fusion | flops 37748736 | bytes 100794368 | tf_op jit(solution)/shard_map/sub | solution.py:68
  449.7 20.6 %fusion.72 = f32[1,128,128,256]{3,2,1,0:T(8,128)} fusion(f32[128,128,128]{1,2,0:T(8,128)} %get-tuple-element.39, f32[128,128,128]{1,2,0:T(8,128)} %get-tuple-element.38, f32[128,128]{1,0:T(8,128)S(1)} %get-tuple-element.88, f32[128,128]{1,0:T(8,128)S(1)} %get-tuple-element.87, f32[128,128]{1,0:T(8,128)S(1)} %fusion.158), kind=kOutput, calls=%fused_computation.84 | convolution fusion | flops 6446841856 | bytes 33751040 | tf_op jit(solution)/shard_map/dot_general | solution.py:73
  470.3 20.3 %fusion.84 = f32[1,128,128,256]{3,2,1,0:T(8,128)} fusion(f32[128,128,128]{1,2,0:T(8,128)} %get-tuple-element.74, f32[128,128,128]{1,2,0:T(8,128)} %get-tuple-element.75, f32[128,128]{1,0:T(8,128)S(1)} %get-tuple-element.88, f32[128,128]{1,0:T(8,128)S(1)} %get-tuple-element.87, f32[128,128]{1,0:T(8,128)S(1)} %fusion.158), kind=kOutput, calls=%fused_computation.88 | convolution fusion | flops 6446841856 | bytes 33751040 | tf_op jit(solution)/shard_map/dot_general | solution.py:73
  490.5 20.4 %fusion.87 = f32[1,128,128,256]{3,2,1,0:T(8,128)} fusion(f32[128,128,128]{1,2,0:T(8,128)} %get-tuple-element.76, f32[128,128,128]{1,2,0:T(8,128)} %get-tuple-element.77, f32[128,128]{1,0:T(8,128)S(1)} %get-tuple-element.88, f32[128,128]{1,0:T(8,128)S(1)} %get-tuple-element.87, f32[128,128]{1,0:T(8,128)S(1)} %fusion.158), kind=kOutput, calls=%fused_computation.89 | convolution fusion | flops 6446841856 | bytes 33751040 | tf_op jit(solution)/shard_map/dot_general | solution.py:73
  510.9 18.9 %multiply_subtract_fusion.5 = (f32[1,128,128,128]{3,2,1,0:T(8,128)}, f32[1,128,128,128]{3,2,1,0:T(8,128)}) fusion(f32[1,128,128,256]{3,2,1,0:T(8,128)} %fusion.72, f32[1,128,128,256]{3,2,1,0:T(8,128)} %fusion.84), kind=kLoop, calls=%fused_computation.110 | loop fusion | flops 14680064 | bytes 50331648 | tf_op jit(solution)/shard_map/sub | solution.py:118
  529.8 30.9 %multiply_subtract_fusion.3 = (f32[1,128,128,128]{3,2,1,0:T(8,128)}, f32[1,128,128,128]{3,2,1,0:T(8,128)}, f32[1,128,128,128]{3,2,1,0:T(8,128)}, f32[1,128,128,128]{3,2,1,0:T(8,128)}) fusion(f32[1,128,128,256]{3,2,1,0:T(8,128)} %fusion.72, f32[1,128,128,256]{3,2,1,0:T(8,128)} %fusion.87, f32[1,128,128,256]{3,2,1,0:T(8,128)} %fusion.84), kind=kLoop, calls=%fused_computation.106 | loop fusion | flops 27262976 | bytes 83886080 | tf_op jit(solution)/shard_map/sub | solution.py:118
  560.7 14.3 %fusion.45 = f32[128,128,256]{1,2,0:T(8,128)} fusion(f32[1,128,128,128]{3,2,1,0:T(8,128)} %get-tuple-element.25, f32[1,128,128,128]{3,2,1,0:T(8,128)} %get-tuple-element.24, f32[128,128]{1,0:T(8,128)S(1)} %get-tuple-element.88, f32[128,128]{1,0:T(8,128)S(1)} %fusion.158, f32[128,128]{1,0:T(8,128)S(1)} %get-tuple-element.87), kind=kOutput, calls=%fused_computation.49 | convolution fusion | flops 6446841856 | bytes 33751040 | tf_op jit(solution)/shard_map/dot_general | solution.py:81
  575.0 13.8 %fusion.52 = f32[128,128,256]{1,2,0:T(8,128)} fusion(f32[1,128,128,128]{3,2,1,0:T(8,128)} %get-tuple-element.21, f32[1,128,128,128]{3,2,1,0:T(8,128)} %get-tuple-element.20, f32[128,128]{1,0:T(8,128)S(1)} %get-tuple-element.88, f32[128,128]{1,0:T(8,128)S(1)} %fusion.158, f32[128,128]{1,0:T(8,128)S(1)} %get-tuple-element.87), kind=kOutput, calls=%fused_computation.57 | convolution fusion | flops 6446841856 | bytes 33751040 | tf_op jit(solution)/shard_map/dot_general | solution.py:81
  588.9 13.0 %fusion.8 = f32[128,128,256]{1,2,0:T(8,128)} fusion(f32[1,128,128,128]{3,2,1,0:T(8,128)S(1)} %bitcast.181, f32[1,128,128,128]{3,2,1,0:T(8,128)} %get-tuple-element.57, f32[128,128]{1,0:T(8,128)S(1)} %get-tuple-element.88, f32[128,128]{1,0:T(8,128)S(1)} %fusion.158, f32[128,128]{1,0:T(8,128)S(1)} %get-tuple-element.87), kind=kOutput, calls=%fused_computation.9 | convolution fusion | flops 6446841856 | bytes 33751040 | tf_op jit(solution)/shard_map/dot_general | solution.py:81
  601.9 31.7 %multiply_add_fusion.2 = (f32[128,128,128]{1,2,0:T(8,128)}, f32[128,128,128]{1,2,0:T(8,128)}, f32[128,128,128]{1,2,0:T(8,128)}, f32[128,128,128]{1,2,0:T(8,128)}...) fusion(f32[128,128,256]{1,2,0:T(8,128)} %fusion.52, f32[128,128]{0,1:T(8,128)S(1)} %copy.407, ...), kind=kLoop, calls=%fused_computation.104 | loop fusion | flops 37748736 | bytes 100794368 | tf_op jit(solution)/shard_map/add | solution.py:89
  633.7 12.8 %fusion.119 = f32[128,64,128]{2,1,0:T(8,128)} fusion(f32[128,128,128]{1,2,0:T(8,128)} %get-tuple-element.68, f32[128,128,128]{1,2,0:T(8,128)} %get-tuple-element.69, f32[64,128]{1,0:T(8,128)S(1)} %copy-done.10, f32[64,128]{1,0:T(8,128)S(1)} %copy-done.8), kind=kOutput, calls=%fused_computation.166 | convolution fusion | flops 1614839808 | bytes 21037056 | tf_op jit(solution)/shard_map/nk,rkm->rnm/dot_general | solution.py:94
  651.9 12.6 %fusion.110 = f32[128,64,128]{2,1,0:T(8,128)} fusion(f32[128,128,128]{1,2,0:T(8,128)} %get-tuple-element.70, f32[128,128,128]{1,2,0:T(8,128)} %get-tuple-element.71, f32[64,128]{1,0:T(8,128)S(1)} %copy-done.10, f32[64,128]{1,0:T(8,128)S(1)} %copy-done.8), kind=kOutput, calls=%fused_computation.163 | convolution fusion | flops 1614839808 | bytes 21037056 | tf_op jit(solution)/shard_map/nk,rkm->rnm/dot_general | solution.py:94
  670.2 10.8 convolution_bitcast_fusion.3
  688.2 20.1 %fusion.81 = f32[1,128,128,256]{3,2,1,0:T(8,128)} fusion(f32[128,128,128]{1,2,0:T(8,128)} %get-tuple-element.47, f32[128,128,128]{1,2,0:T(8,128)} %get-tuple-element.46, f32[128,128]{1,0:T(8,128)S(1)} %get-tuple-element.88, f32[128,128]{1,0:T(8,128)S(1)} %get-tuple-element.87, f32[128,128]{1,0:T(8,128)S(1)} %fusion.158), kind=kOutput, calls=%fused_computation.87 | convolution fusion | flops 6446841856 | bytes 33751040 | tf_op jit(solution)/shard_map/dot_general | solution.py:73
  708.3 30.8 %multiply_subtract_fusion.1 = (f32[1,128,128,128]{3,2,1,0:T(8,128)}, f32[1,128,128,128]{3,2,1,0:T(8,128)}, f32[1,128,128,128]{3,2,1,0:T(8,128)}, f32[1,128,128,128]{3,2,1,0:T(8,128)}) fusion(f32[1,128,128,256]{3,2,1,0:T(8,128)} %fusion.75, f32[1,128,128,256]{3,2,1,0:T(8,128)} %fusion.81, f32[1,128,128,256]{3,2,1,0:T(8,128)} %fusion.78), kind=kLoop, calls=%fused_computation.102 | loop fusion | flops 27262976 | bytes 83886080 | tf_op jit(solution)/shard_map/sub | solution.py:118
  739.1 14.3 %fusion.59 = f32[128,128,256]{1,2,0:T(8,128)} fusion(f32[1,128,128,128]{3,2,1,0:T(8,128)} %get-tuple-element.23, f32[1,128,128,128]{3,2,1,0:T(8,128)} %get-tuple-element.22, f32[128,128]{1,0:T(8,128)S(1)} %get-tuple-element.88, f32[128,128]{1,0:T(8,128)S(1)} %fusion.158, f32[128,128]{1,0:T(8,128)S(1)} %get-tuple-element.87), kind=kOutput, calls=%fused_computation.65 | convolution fusion | flops 6446841856 | bytes 33751040 | tf_op jit(solution)/shard_map/dot_general | solution.py:81
  753.5 12.9 %fusion.23 = f32[128,128,256]{1,2,0:T(8,128)} fusion(f32[1,128,128,128]{3,2,1,0:T(8,128)S(1)} %copy-done, f32[1,128,128,128]{3,2,1,0:T(8,128)} %get-tuple-element.59, f32[128,128]{1,0:T(8,128)S(1)} %get-tuple-element.88, f32[128,128]{1,0:T(8,128)S(1)} %fusion.158, f32[128,128]{1,0:T(8,128)S(1)} %get-tuple-element.87), kind=kOutput, calls=%fused_computation.25 | convolution fusion | flops 6446841856 | bytes 33751040 | tf_op jit(solution)/shard_map/dot_general | solution.py:81
  766.4 22.5 %multiply_add_fusion = (f32[128,128,128]{1,2,0:T(8,128)}, f32[128,128,128]{1,2,0:T(8,128)}, f32[128,128,128]{1,2,0:T(8,128)S(1)}, f32[128,128,128]{1,2,0:T(8,128)}) fusion(f32[128,128,256]{1,2,0:T(8,128)} %fusion.59, f32[128,128]{0,1:T(8,128)S(1)} %copy.407, f32[128,128]{0,1:T(8,128)S(1)} %copy.406, f32[128,128,256]{1,2,0:T(8,128)} %fusion.23), kind=kLoop, calls=%fused_computation.100 | loop fusion | flops 25165824 | bytes 67239936 | tf_op jit(solution)/shard_map/add | solution.py:89
  788.9 11.4 fusion.116
  805.9 12.2 %add_convert_fusion = (bf16[1,1,128,8192]{2,3,0,1:T(8,128)(2,1)}, bf16[1,1,128,8192]{2,3,0,1:T(8,128)(2,1)}, bf16[1,1,128,8192]{2,3,0,1:T(8,128)(2,1)}, bf16[1,1,128,8192]{2,3,0,1:T(8,128)(2,1)S(1)}) fusion(f32[1,1,128,8192]{2,3,0,1:T(8,128)} %bitcast.197, f32[1,1,128,8192]{2,3,0,1:T(8,128)} %bitcast.195, bf16[1,1,128,8192]{2,3,0,1:T(8,128)(2,1)S(1)} %copy-done.3, ...), kind=kLoop, calls=%fused_computation.147 | loop fusion | flops 20971520 | bytes 35652608 | tf_op jit(solution)/shard_map/convert_element_type | solution.py:202
  820.2 33.3 %copy.501 = bf16[1,1,8192,128]{3,1,0,2:T(2,128)(2,1)} copy(bf16[1,1,8192,128]{3,2,0,1:T(8,128)(2,1)S(1)} %fusion.122) | data formatting | bytes 4194304 | tf_op jit(solution)/shard_map/transpose | solution.py:135
  853.4 45.1 %reduce.1 = bf16[8192,128]{1,0:T(8,128)(2,1)S(1)} reduce(bf16[8192,1,1,128]{3,2,1,0:T(2,128)(2,1)} %bitcast.200, bf16[]{:T(256)} %broadcast.130), dimensions={1,2}, to_apply=%bitcast.174.reduce_sub_computation | reduce | bytes 4194306
  901.7 32.6 %all_to_all.63 = bf16[8,2,65536]{2,1,0:T(2,128)(2,1)S(1)} all-to-all(bf16[8,2,65536]{2,1,0:T(2,128)(2,1)} %reshape.355), channel_id=1, replica_groups=mesh['seq'=8,'tp'=4] {'seq'}, dimensions={0} | all-to-all | bytes 4194304 | tf_op jit(solution)/shard_map/all_to_all | solution.py:135
  943.7 14.9 %convert_bitcast_fusion = bf16[4096,1024]{0,1:T(8,128)(2,1)} fusion(bf16[1024,1024]{0,1:T(8,128)(2,1)} %bitcast.206, bf16[1024,4096]{1,0:T(8,128)(2,1)} %param.10), kind=kOutput, calls=%fused_computation.119 | convolution fusion | flops 8594128896 | bytes 18874368 | tf_op jit(solution)/shard_map/dot_general | solution.py:171
  963.4 40.0 %copy.441 = bf16[3,1,8192,128]{3,0,1,2:T(4,128)(2,1)} copy(bf16[3,1,8192,128]{3,2,0,1:T(8,128)(2,1)S(1)} %maximum_bitcast_fusion.12) | data formatting | bytes 12582912 | tf_op jit(solution)/shard_map/transpose | solution.py:135
  1009.9 12.7 %fusion.107 = f32[128,64,128]{2,1,0:T(8,128)} fusion(f32[128,128,128]{1,2,0:T(8,128)} %get-tuple-element.33, f32[128,128,128]{1,2,0:T(8,128)} %get-tuple-element.32, f32[64,128]{1,0:T(8,128)S(1)} %copy-done.10, f32[64,128]{1,0:T(8,128)S(1)} %copy-done.8), kind=kOutput, calls=%fused_computation.162 | convolution fusion | flops 1614839808 | bytes 21037056 | tf_op jit(solution)/shard_map/nk,rkm->rnm/dot_general | solution.py:94
  1027.7 12.9 %fusion.104 = f32[128,64,128]{2,1,0:T(8,128)} fusion(f32[128,128,128]{1,2,0:T(8,128)} %get-tuple-element.35, f32[128,128,128]{1,2,0:T(8,128)} %get-tuple-element.34, f32[64,128]{1,0:T(8,128)S(1)} %copy-done.10, f32[64,128]{1,0:T(8,128)S(1)} %copy-done.8), kind=kOutput, calls=%fused_computation.161 | convolution fusion | flops 1614839808 | bytes 21037056 | tf_op jit(solution)/shard_map/nk,rkm->rnm/dot_general | solution.py:94
  1045.6 54.8 %all-to-all-done.3 = bf16[3,1,8192,128]{3,0,1,2:T(4,128)(2,1)} async-done(((bf16[3,1,8192,128]{3,0,1,2:T(4,128)(2,1)}), bf16[3,1,8192,128]{3,0,1,2:T(4,128)(2,1)}, u32[]{:S(2)}, u32[]{:S(2)}) %all-to-all-start.3) | async-done | bytes 6291488 | tf_op jit(solution)/shard_map/all_to_all | solution.py:135
  1107.4 8.7 copy.443
  1137.0 11.5 fusion.67
  (112 shorter events, 203.3 us)
Async XLA Ops:
  7.2 172.1 %all-gather.2.cloned.1.call-start = ((), (), s32[]{:S(2)}) async-start(), calls=%async_computation.6 | async-start | bytes 10485760 | tf_op jit(solution)/shard_map/all_gather | solution.py:180
  8.7 14.4 %collective-permute-start = (bf16[1,2,3,1024]{3,1,2,0:T(2,128)(2,1)S(1)}, bf16[1,2,3,1024]{3,1,2,0:T(2,128)(2,1)S(1)}, u32[]{:S(2)}, u32[]{:S(2)}) collective-permute-start(bf16[1,2,3,1024]{3,1,2,0:T(2,128)(2,1)S(1)} %slice.194), channel_id=1, source_target_pairs={{0,4},{4,8},{8,12},{12,16},{16,20},{20,24},{24,28},{1,5},{5,9},{9,... | collective-permute-start | bytes 36872 | tf_op jit(solution)/shard_map/ppermute | solution.py:15
  14.2 20.8 %copy-start.11 = (f32[3,1024]{1,0:T(4,128)}, f32[3,1024]{1,0:T(4,128)S(1)}, u32[]{:S(2)}) copy-start(f32[3,1024]{1,0:T(4,128)S(1)} %get-tuple-element.85) | copy-start | bytes 36868
  14.2 20.7 %copy-start.13 = (f32[3,1024]{1,0:T(4,128)}, f32[3,1024]{1,0:T(4,128)S(1)}, u32[]{:S(2)}) copy-start(f32[3,1024]{1,0:T(4,128)S(1)} %get-tuple-element.86) | copy-start | bytes 36868
  23.1 11.9 %copy-start.15 = (f32[3,1,1024]{2,0,1:T(4,128)}, f32[3,1,1024]{2,0,1:T(4,128)S(1)}, u32[]{:S(2)}) copy-start(f32[3,1,1024]{2,0,1:T(4,128)S(1)} %copy.500) | copy-start | bytes 36868
  67.9 94.1 %all-to-all-start = ((bf16[3,1,1024,1024]{2,0,1,3:T(4,128)(2,1)}), bf16[3,1,1024,1024]{2,0,1,3:T(4,128)(2,1)}, u32[]{:S(2)}, u32[]{:S(2)}) async-start(bf16[3,1,1024,1024]{2,0,1,3:T(4,128)(2,1)} %copy.401), calls=%async_computation | async-start | bytes 16777216 | tf_op jit(solution)/shard_map/all_to_all | solution.py:130
  78.7 1.8 copy-start.20
  81.1 307.7 %copy-start.9 = (f32[64,128]{1,0:T(8,128)}, f32[64,128]{1,0:T(8,128)S(1)}, u32[]{:S(2)}) copy-start(f32[64,128]{1,0:T(8,128)S(1)} %slice_negate_fusion.1) | copy-start | bytes 98308
  81.1 322.3 %copy-start.5 = (f32[128,64]{1,0:T(8,128)}, f32[128,64]{1,0:T(8,128)S(1)}, u32[]{:S(2)}) copy-start(f32[128,64]{1,0:T(8,128)S(1)} %slice_negate_fusion) | copy-start | bytes 98308
  217.7 30.6 %all-to-all-start.2 = ((bf16[8,2,65536]{2,1,0:T(2,128)(2,1)}), bf16[8,2,65536]{2,1,0:T(2,128)(2,1)}, u32[]{:S(2)}, u32[]{:S(2)}) async-start(bf16[8,2,65536]{2,1,0:T(2,128)(2,1)} %reshape.357), calls=%async_computation.3 | async-start | bytes 4194304 | tf_op jit(solution)/shard_map/all_to_all | solution.py:130
  225.1 932.0 %reduce-scatter.2.cloned.1.call-start = ((), (), s32[]{:S(2)}) async-start(), calls=%async_computation.5 | async-start | bytes 10485760 | tf_op jit(solution)/shard_map/reduce_scatter | solution.py:170
  234.0 14.3 %copy-start.1 = (bf16[128,64,128]{2,1,0:T(8,128)(2,1)}, bf16[128,64,128]{2,1,0:T(8,128)(2,1)S(1)}, u32[]{:S(2)}) copy-start(bf16[128,64,128]{2,1,0:T(8,128)(2,1)S(1)} %copy.477) | copy-start | bytes 6291460
  381.6 7.2 copy-start.7
  397.9 5.4 copy-start.17
  560.7 28.2 %slice-start = ((s8[8388608]{0:T(1024)(128)(4,1)}), s8[4194304]{0:T(1024)(128)(4,1)S(1)}, s32[]{:S(2)}) async-start(s8[8388608]{0:T(1024)(128)(4,1)} %bitcast.180), calls=%async_computation.7 | async-start | bytes 8388608
  575.0 13.8 %slice-start.1 = ((s8[8388608]{0:T(1024)(128)(4,1)}), s8[4194304]{0:T(1024)(128)(4,1)S(1)}, s32[]{:S(2)}) async-start(s8[8388608]{0:T(1024)(128)(4,1)} %bitcast.180), calls=%async_computation.8 | async-start | bytes 8388608
  601.9 31.7 %copy-start.8 = (f32[64,128]{1,0:T(8,128)S(1)}, f32[64,128]{1,0:T(8,128)}, u32[]{:S(2)}) copy-start(f32[64,128]{1,0:T(8,128)} %slice.271) | copy-start | bytes 98308
  601.9 31.7 %copy-start.10 = (f32[64,128]{1,0:T(8,128)S(1)}, f32[64,128]{1,0:T(8,128)}, u32[]{:S(2)}) copy-start(f32[64,128]{1,0:T(8,128)} %copy-done.9) | copy-start | bytes 98308
  664.6 5.6 copy-start.2
  664.6 5.6 copy-start.6
  664.6 5.6 copy-start.19
  739.1 14.3 %copy-start = (f32[1,128,128,128]{3,2,1,0:T(8,128)S(1)}, f32[1,128,128,128]{3,2,1,0:T(8,128)}, u32[]{:S(2)}) copy-start(f32[1,128,128,128]{3,2,1,0:T(8,128)} %get-tuple-element.58) | copy-start | bytes 25165828
  800.3 5.6 copy-start.3
  800.3 5.6 copy-start.18
  958.6 1.6 copy-start.4
  1003.4 97.0 %all-to-all-start.3 = ((bf16[3,1,8192,128]{3,0,1,2:T(4,128)(2,1)}), bf16[3,1,8192,128]{3,0,1,2:T(4,128)(2,1)}, u32[]{:S(2)}, u32[]{:S(2)}) async-start(bf16[3,1,8192,128]{3,0,1,2:T(4,128)(2,1)} %copy.441), calls=%async_computation.4 | async-start | bytes 16777216 | tf_op jit(solution)/shard_map/all_to_all | solution.py:135
  1117.6 13.6 %collective-permute-start.1 = (bf16[1,2,3,1024]{3,1,2,0:T(2,128)(2,1)S(1)}, bf16[1,2,3,1024]{3,1,2,0:T(2,128)(2,1)S(1)}, u32[]{:S(2)}, u32[]{:S(2)}) collective-permute-start(bf16[1,2,3,1024]{3,1,2,0:T(2,128)(2,1)S(1)} %copy.444), channel_id=1, source_target_pairs={{4,0},{8,4},{12,8},{16,12},{20,16},{24,20},{28,24},{5,1},{9,5},{13... | collective-permute-start | bytes 36872 | tf_op jit(solution)/shard_map/ppermute | solution.py:15
  1132.3 4.6 copy-start.12
  1132.4 4.6 copy-start.14
  1132.4 4.6 copy-start.16
Sparse Core Ops, SparseCore 0:
  9.5 151.8 all-gather.1
  958.8 144.7 reduce-scatter.1
where the time goes:
time: 1170 us; the launch traced here: 1160 us
  other arithmetic  369 us (32%)
  matrix products  366 us (31%)
  local copies, waits for them, and re-layouts  236 us (20%)
  waiting for transfers between devices  117 us (10%)
  blocking collectives  32.6 us (3%)
  starting transfers between devices  29.1 us (2%)
  between operations  14.6 us (1%)
    dot_general x6, matrix products, forward_dft(): jnp.dot(turned.reshape(row_count * outer, 2 * inner), forward_mix, precis...  122 us
    sub x4, other arithmetic, spectral_product(): left_real * right_real - left_imag * right_imag  99.5 us
    dot_general x6, matrix products, inverse_dft(): jnp.dot(spectrum.reshape(row_count * outer, 2 * inner), inverse_mix, prec...  82.5 us
    transpose x2, local copies, waits for them, and re-layouts, to_frames(): jnp.swapaxes(block, 2, 3)  73.3 us
    dot_general x6, matrix products, inverse_dft(): signal = jnp.einsum('nk,rkm->rnm', closing, turned, precision=precise)  71.7 us
    sub x3, other arithmetic, forward_dft(): real_part * twist_real - imag_part * twist_imag  64.9 us
    all_to_all x2, waiting for transfers between devices, to_channels(): lax.all_to_all(block, 'seq', split_axis=3, concat_axis=2, tiled=True)  61.5 us
    add x3, other arithmetic, inverse_dft(): real_part * twist_real + imag_part * twist_imag  61.3 us
  transfers between devices with their start and end apart: 7, of which 2 were waited for; matrix products, arithmetic and copies ran while one was open for 22% of the time, Pallas kernels for 0%

commit v1 on v0

--- a/solution.py
+++ b/solution.py
@@ -7,6 +7,13 @@
 LEN = 8192
 SEQS = 1
 precise = lax.Precision.HIGH
+
+
+def swap_blocks(x, mesh_axis, split, join):
+    size = lax.axis_size(mesh_axis)
+    blocks = jnp.stack(jnp.split(x, size, axis=split), axis=0)
+    blocks = lax.all_to_all(blocks, mesh_axis, split_axis=0, concat_axis=0)
+    return jnp.concatenate(blocks, axis=join)
 
 
 def from_behind(block, axis, distance):
@@ -132,7 +139,7 @@
 
 
 def to_frames(block):
-    return lax.all_to_all(jnp.swapaxes(block, 2, 3), "seq", split_axis=2, concat_axis=3, tiled=True)
+    return swap_blocks(jnp.swapaxes(block, 2, 3), "seq", 2, 3)
 
 
 def local(projected, short_kernel, filters, skip_gain, out_weight, out_grad):

time: 1170 us -> 1060 us (0.906)
  local copies, waits for them, and re-layouts: 236 us -> 148 us
  waiting for transfers between devices: 117 us -> 98.4 us
    transpose x3 -> x0, local copies, waits for them, and re-layouts: 84.8 us -> none  [the longest x2 73.3 us: to_frames(): jnp.swapaxes(block, 2, 3)]
    all_gather x1, waiting for transfers between devices: 0.01 us -> 65 us  [local(): lax.all_gather(out_grad, 'tp', axis=2, tiled=True)]
    all_to_all x2, waiting for transfers between devices: 61.5 us -> 0.01 us  [to_channels(): lax.all_to_all(block, 'seq', split_axis=3, concat_axis=2, tiled=True)]
    unnamed x3, other arithmetic: 57.8 us -> 15.5 us
    all_to_all x1, waiting for transfers between devices: 54.8 us -> 32.7 us  [swap_blocks(): blocks = lax.all_to_all(blocks, mesh_axis, split_axis=0, concat_axis=0)]
    convert_element_type x1, other arithmetic: 11.5 us -> 33 us  [local(): projected_grad = sum((short_kernel[:, offset, :] * tail[:, offset:offset...]
    all_to_all x3 -> x0, local copies, waits for them, and re-layouts: 18.3 us -> none  [to_frames(): lax.all_to_all(jnp.swapaxes(block, 2, 3), 'seq', split_axis=2, concat_axi...]
    unnamed x59 -> x75, local copies, waits for them, and re-layouts: 45.7 us -> 57.7 us
  transfers between devices with their start and end apart: 7 -> 7, of which waited for: 2 -> 2; matrix products, arithmetic and copies ran while one was open for 22% -> 27% of each run, Pallas kernels for 0% -> 0%
where the time goes in v1:
time: 1060 us; the launch traced here: 1050 us
  other arithmetic  367 us (35%)
  matrix products  367 us (35%)
  local copies, waits for them, and re-layouts  148 us (14%)
  waiting for transfers between devices  98.4 us (9%)
  blocking collectives  29.4 us (3%)
  starting transfers between devices  25.4 us (2%)
  between operations  14.7 us (1%)
    dot_general x6, matrix products, forward_dft(): jnp.dot(turned.reshape(row_count * outer, 2 * inner), forward_mix, precis...  122 us
    sub x4, other arithmetic, spectral_product(): left_real * right_real - left_imag * right_imag  99.5 us
    dot_general x6, matrix products, inverse_dft(): jnp.dot(spectrum.reshape(row_count * outer, 2 * inner), inverse_mix, prec...  82.2 us
    dot_general x6, matrix products, inverse_dft(): signal = jnp.einsum('nk,rkm->rnm', closing, turned, precision=precise)  75.9 us
    all_gather x1, waiting for transfers between devices, local(): lax.all_gather(out_grad, 'tp', axis=2, tiled=True)  65 us
    sub x3, other arithmetic, forward_dft(): real_part * twist_real - imag_part * twist_imag  64.8 us
    add x3, other arithmetic, inverse_dft(): real_part * twist_real + imag_part * twist_imag  63.8 us
    dot_general x6, matrix products, forward_dft(): mixed = jnp.einsum('kn,rnm->rkm', opening, shaped, precision=precise)  59.1 us
  transfers between devices with their start and end apart: 7, of which 2 were waited for; matrix products, arithmetic and copies ran while one was open for 27% of the time, Pallas kernels for 0%

profile of v1, /device:TPU:1, one launch (start us, length us, event | category | flops | bytes accessed | tf_op | source)
XLA Modules:
  0.0 1050.7 jit_solution(17683624733207946158)
XLA Ops:
  14.2 14.6 %copy.235 = bf16[1,1024,3,1024]{1,2,0,3:T(4,128)(2,1)} copy(bf16[1,1024,3,1024]{3,1,2,0:T(8,128)(2,1)} %param.6) | data formatting | bytes 12582912 | tf_op args[0]
  30.3 10.9 %maximum_convert_fusion = f32[1,1026,3,1024]{1,2,0,3:T(4,128)} fusion(bf16[1,1024,3,1024]{1,2,0,3:T(4,128)(2,1)} %copy.235, bf16[1,2,3,1024]{1,2,0,3:T(4,128)(2,1)S(1)} %copy.234), kind=kLoop, calls=%fused_computation.84 | loop fusion | flops 12607488 | bytes 18911232 | tf_op jit(solution)/shard_map/convert_element_type | solution.py:149
  41.2 29.8 %fusion.92 = bf16[3,1,1024,1024]{2,0,1,3:T(4,128)(2,1)} fusion(f32[1,1026,3,1024]{1,2,0,3:T(4,128)} %maximum_convert_fusion, f32[3,1024]{0,1:T(8,128)S(1)} %bitcast.282, f32[3,1024]{0,1:T(8,128)S(1)} %bitcast.284, f32[3,1024]{0,1:T(8,128)S(1)} %bitcast.280), kind=kLoop, calls=%fused_computation.138 | loop fusion | flops 18874368 | bytes 44077056 | tf_op jit(solution)/shard_map/transpose | solution.py:156
  86.7 9.7 convolution_bitcast_fusion.2
  96.4 65.0 %all-gather.2.cloned.1.call-done = bf16[1,1024,4096]{2,1,0:T(8,128)(2,1)} async-done(((bf16[1,1024,1024]{2,1,0:T(8,128)(2,1)}), bf16[1,1024,4096]{2,1,0:T(8,128)(2,1)}) %all-gather.2.cloned.1.call-update) | async-done | bytes 8388624 | tf_op jit(solution)/shard_map/all_gather | solution.py:187
  161.4 13.7 %convert_bitcast_fusion.3 = bf16[1,1,1024,1024]{3,2,1,0:T(8,128)(2,1)S(1)} fusion(bf16[1024,4096]{1,0:T(8,128)(2,1)} %param.10, bf16[1,1024,4096]{2,1,0:T(8,128)(2,1)} %all-gather.2.cloned.1.call-done), kind=kOutput, calls=%fused_computation.172 | convolution fusion | flops 8590983168 | bytes 18874368 | tf_op jit(solution)/shard_map/dot_general | solution.py:186
  183.2 12.8 %reduce = bf16[1024,1024]{1,0:T(8,128)(2,1)S(1)} reduce(bf16[1024,1,1,1024]{3,2,1,0:T(2,128)(2,1)} %bitcast.278, bf16[]{:T(256)} %broadcast.130), dimensions={1,2}, to_apply=%bitcast.243.reduce_sub_computation | reduce | bytes 4194306
  204.1 11.8 %convolution_bitcast_fusion.4 = f32[128,256,128]{1,2,0:T(8,128)} fusion(f32[128,64,128]{2,1,0:T(8,128)} %bitcast.267, f32[128,64]{1,0:T(8,128)S(1)} %slice_negate_fusion, f32[128,64]{1,0:T(8,128)S(1)} %bitcast.270), kind=kOutput, calls=%fused_computation.96 | convolution fusion | flops 1610629120 | bytes 21037056 | tf_op jit(solution)/shard_map/kn,rnm->rkm/dot_general | solution.py:70
  216.0 10.7 %copy.238 = bf16[3,1,8,1024,128]{3,2,4,0,1:T(8,128)(2,1)} copy(bf16[3,1,8,1024,128]{3,0,4,2,1:T(4,128)(2,1)} %bitcast.7) | data formatting | bytes 12582912 | tf_op jit(solution)/shard_map/all_to_all | solution.py:137
  226.6 10.4 all_to_all.31
  243.2 8.5 convolution_bitcast_fusion.5
  289.6 25.6 %multiply_subtract_fusion.9 = (f32[128,128,128]{1,2,0:T(8,128)}, f32[128,128,128]{1,2,0:T(8,128)}, f32[128,128,128]{1,2,0:T(8,128)}, f32[128,128,128]{1,2,0:T(8,128)}) fusion(f32[128,256,128]{1,2,0:T(8,128)} %convolution_bitcast_fusion.1, f32[128,128]{0,1:T(8,128)S(1)} %copy.241, f32[128,128]{0,1:T(8,128)S(1)} %copy.240, ...), kind=kLoop, calls=%fused_computation.120 | loop fusion | flops 25165824 | bytes 67239936 | tf_op jit(solution)/shard_map/sub | solution.py:75
  315.2 20.2 %fusion.75 = f32[1,128,128,256]{3,2,1,0:T(8,128)} fusion(f32[128,128,128]{1,2,0:T(8,128)} %get-tuple-element.37, f32[128,128,128]{1,2,0:T(8,128)} %get-tuple-element.36, f32[128,128]{1,0:T(8,128)S(1)} %get-tuple-element.86, f32[128,128]{1,0:T(8,128)S(1)} %get-tuple-element.85, f32[128,128]{1,0:T(8,128)S(1)} %fusion.172), kind=kOutput, calls=%fused_computation.87 | convolution fusion | flops 6446841856 | bytes 33751040 | tf_op jit(solution)/shard_map/dot_general | solution.py:80
  335.4 20.3 %fusion.78 = f32[1,128,128,256]{3,2,1,0:T(8,128)} fusion(f32[128,128,128]{1,2,0:T(8,128)} %get-tuple-element.74, f32[128,128,128]{1,2,0:T(8,128)} %get-tuple-element.75, f32[128,128]{1,0:T(8,128)S(1)} %get-tuple-element.86, f32[128,128]{1,0:T(8,128)S(1)} %get-tuple-element.85, f32[128,128]{1,0:T(8,128)S(1)} %fusion.172), kind=kOutput, calls=%fused_computation.88 | convolution fusion | flops 6446841856 | bytes 33751040 | tf_op jit(solution)/shard_map/dot_general | solution.py:80
  355.7 18.9 %multiply_subtract_fusion.8 = (f32[1,128,128,128]{3,2,1,0:T(8,128)}, f32[1,128,128,128]{3,2,1,0:T(8,128)}) fusion(f32[1,128,128,256]{3,2,1,0:T(8,128)} %fusion.75, f32[1,128,128,256]{3,2,1,0:T(8,128)} %fusion.78), kind=kLoop, calls=%fused_computation.118 | loop fusion | flops 14680064 | bytes 50331648 | tf_op jit(solution)/shard_map/sub | solution.py:125
  374.6 14.2 %fusion.40 = f32[128,128,256]{1,2,0:T(8,128)} fusion(f32[1,128,128,128]{3,2,1,0:T(8,128)} %get-tuple-element.21, f32[1,128,128,128]{3,2,1,0:T(8,128)} %get-tuple-element.20, f32[128,128]{1,0:T(8,128)S(1)} %get-tuple-element.86, f32[128,128]{1,0:T(8,128)S(1)} %fusion.172, f32[128,128]{1,0:T(8,128)S(1)} %get-tuple-element.85), kind=kOutput, calls=%fused_computation.49 | convolution fusion | flops 6446841856 | bytes 33751040 | tf_op jit(solution)/shard_map/dot_general | solution.py:88
  388.8 9.6 multiply_add_fusion.7
  398.4 12.3 %bitcast_multiply_fusion = (f32[128,64,128]{2,1,0:T(8,128)}, f32[128,64,128]{2,1,0:T(8,128)}) fusion(f32[16,8,64,128]{3,2,1,0:T(8,128)S(1)} %copy-done, f32[128]{0:T(128)S(1)} %copy-done.19, bf16[16,8,64,128]{3,2,1,0:T(8,128)(2,1)S(1)} %copy.321, f32[64,128]{1,0:T(8,128)S(1)} %copy-done.17, f32[64,128]{1,0:T(8,128)S(1)} %copy-done.15, ...), kind=kOutput, calls=%fused_computation.155 | convolution fusion | flops 1619034112 | bytes 31523328 | tf_op jit(solution)/shard_map/nk,rkm->rnm/dot_general | solution.py:101
  415.7 12.0 %convolution_bitcast_fusion = f32[128,256,128]{1,2,0:T(8,128)} fusion(f32[128,64,128]{2,1,0:T(8,128)} %get-tuple-element.81, f32[128,64]{1,0:T(8,128)S(1)} %slice_negate_fusion, f32[128,64]{1,0:T(8,128)S(1)} %bitcast.273), kind=kOutput, calls=%fused_computation.92 | convolution fusion | flops 1610629120 | bytes 21037056 | tf_op jit(solution)/shard_map/kn,rnm->rkm/dot_general | solution.py:70
  427.8 32.0 %multiply_subtract_fusion.6 = (f32[128,128,128]{1,2,0:T(8,128)}, f32[128,128,128]{1,2,0:T(8,128)}, f32[128,128,128]{1,2,0:T(8,128)}, f32[128,128,128]{1,2,0:T(8,...) fusion(f32[128,256,128]{1,2,0:T(8,128)} %convolution_bitcast_fusion, f32[128,128]{0,1:T(8,128)S(1)} %copy.241, ...), kind=kLoop, calls=%fused_computation.114 | loop fusion | flops 37748736 | bytes 100794368 | tf_op jit(solution)/shard_map/sub | solution.py:75
  459.8 20.1 %fusion.72 = f32[1,128,128,256]{3,2,1,0:T(8,128)} fusion(f32[128,128,128]{1,2,0:T(8,128)} %get-tuple-element.33, f32[128,128,128]{1,2,0:T(8,128)} %get-tuple-element.32, f32[128,128]{1,0:T(8,128)S(1)} %get-tuple-element.86, f32[128,128]{1,0:T(8,128)S(1)} %get-tuple-element.85, f32[128,128]{1,0:T(8,128)S(1)} %fusion.172), kind=kOutput, calls=%fused_computation.86 | convolution fusion | flops 6446841856 | bytes 33751040 | tf_op jit(solution)/shard_map/dot_general | solution.py:80
  479.9 20.5 %fusion.84 = f32[1,128,128,256]{3,2,1,0:T(8,128)} fusion(f32[128,128,128]{1,2,0:T(8,128)} %get-tuple-element.70, f32[128,128,128]{1,2,0:T(8,128)} %get-tuple-element.71, f32[128,128]{1,0:T(8,128)S(1)} %get-tuple-element.86, f32[128,128]{1,0:T(8,128)S(1)} %get-tuple-element.85, f32[128,128]{1,0:T(8,128)S(1)} %fusion.172), kind=kOutput, calls=%fused_computation.90 | convolution fusion | flops 6446841856 | bytes 33751040 | tf_op jit(solution)/shard_map/dot_general | solution.py:80
  500.4 20.2 %fusion.87 = f32[1,128,128,256]{3,2,1,0:T(8,128)} fusion(f32[128,128,128]{1,2,0:T(8,128)} %get-tuple-element.72, f32[128,128,128]{1,2,0:T(8,128)} %get-tuple-element.73, f32[128,128]{1,0:T(8,128)S(1)} %get-tuple-element.86, f32[128,128]{1,0:T(8,128)S(1)} %get-tuple-element.85, f32[128,128]{1,0:T(8,128)S(1)} %fusion.172), kind=kOutput, calls=%fused_computation.91 | convolution fusion | flops 6446841856 | bytes 33751040 | tf_op jit(solution)/shard_map/dot_general | solution.py:80
  520.6 18.9 %multiply_subtract_fusion.5 = (f32[1,128,128,128]{3,2,1,0:T(8,128)}, f32[1,128,128,128]{3,2,1,0:T(8,128)}) fusion(f32[1,128,128,256]{3,2,1,0:T(8,128)} %fusion.72, f32[1,128,128,256]{3,2,1,0:T(8,128)} %fusion.84), kind=kLoop, calls=%fused_computation.112 | loop fusion | flops 14680064 | bytes 50331648 | tf_op jit(solution)/shard_map/sub | solution.py:125
  539.5 30.9 %multiply_subtract_fusion.3 = (f32[1,128,128,128]{3,2,1,0:T(8,128)}, f32[1,128,128,128]{3,2,1,0:T(8,128)}, f32[1,128,128,128]{3,2,1,0:T(8,128)}, f32[1,128,128,128]{3,2,1,0:T(8,128)}) fusion(f32[1,128,128,256]{3,2,1,0:T(8,128)} %fusion.72, f32[1,128,128,256]{3,2,1,0:T(8,128)} %fusion.87, f32[1,128,128,256]{3,2,1,0:T(8,128)} %fusion.84), kind=kLoop, calls=%fused_computation.108 | loop fusion | flops 27262976 | bytes 83886080 | tf_op jit(solution)/shard_map/sub | solution.py:125
  570.5 14.1 %fusion.51 = f32[128,128,256]{1,2,0:T(8,128)} fusion(f32[1,128,128,128]{3,2,1,0:T(8,128)} %get-tuple-element.19, f32[1,128,128,128]{3,2,1,0:T(8,128)} %get-tuple-element.18, f32[128,128]{1,0:T(8,128)S(1)} %get-tuple-element.86, f32[128,128]{1,0:T(8,128)S(1)} %fusion.172, f32[128,128]{1,0:T(8,128)S(1)} %get-tuple-element.85), kind=kOutput, calls=%fused_computation.61 | convolution fusion | flops 6446841856 | bytes 33751040 | tf_op jit(solution)/shard_map/dot_general | solution.py:88
  584.5 13.8 %fusion.58 = f32[128,128,256]{1,2,0:T(8,128)} fusion(f32[1,128,128,128]{3,2,1,0:T(8,128)} %get-tuple-element.15, f32[1,128,128,128]{3,2,1,0:T(8,128)} %get-tuple-element.14, f32[128,128]{1,0:T(8,128)S(1)} %get-tuple-element.86, f32[128,128]{1,0:T(8,128)S(1)} %fusion.172, f32[128,128]{1,0:T(8,128)S(1)} %get-tuple-element.85), kind=kOutput, calls=%fused_computation.69 | convolution fusion | flops 6446841856 | bytes 33751040 | tf_op jit(solution)/shard_map/dot_general | solution.py:88
  598.4 13.1 %fusion.14 = f32[128,128,256]{1,2,0:T(8,128)} fusion(f32[1,128,128,128]{3,2,1,0:T(8,128)S(1)} %bitcast.266, f32[1,128,128,128]{3,2,1,0:T(8,128)} %get-tuple-element.51, f32[128,128]{1,0:T(8,128)S(1)} %get-tuple-element.86, f32[128,128]{1,0:T(8,128)S(1)} %fusion.172, f32[128,128]{1,0:T(8,128)S(1)} %get-tuple-element.85), kind=kOutput, calls=%fused_computation.21 | convolution fusion | flops 6446841856 | bytes 33751040 | tf_op jit(solution)/shard_map/dot_general | solution.py:88
  611.4 31.7 %multiply_add_fusion.2 = (f32[128,128,128]{1,2,0:T(8,128)}, f32[128,128,128]{1,2,0:T(8,128)}, f32[128,128,128]{1,2,0:T(8,128)}, f32[128,128,128]{1,2,0:T(8,128)}...) fusion(f32[128,128,256]{1,2,0:T(8,128)} %fusion.58, f32[128,128]{0,1:T(8,128)S(1)} %copy.241, ...), kind=kLoop, calls=%fused_computation.106 | loop fusion | flops 37748736 | bytes 100794368 | tf_op jit(solution)/shard_map/add | solution.py:96
  643.2 12.9 %fusion.110 = f32[128,64,128]{2,1,0:T(8,128)} fusion(f32[128,128,128]{1,2,0:T(8,128)} %get-tuple-element.66, f32[128,128,128]{1,2,0:T(8,128)} %get-tuple-element.67, f32[64,128]{1,0:T(8,128)S(1)} %copy-done.18, f32[64,128]{1,0:T(8,128)S(1)} %copy-done.16), kind=kOutput, calls=%fused_computation.167 | convolution fusion | flops 1614839808 | bytes 21037056 | tf_op jit(solution)/shard_map/nk,rkm->rnm/dot_general | solution.py:101
  661.2 13.9 %bitcast_multiply_fusion.1 = (f32[128,64,128]{2,1,0:T(8,128)}, f32[128,64,128]{2,1,0:T(8,128)}) fusion(f32[16,8,64,128]{3,2,1,0:T(8,128)} %copy.319, f32[128]{0:T(128)S(1)} %copy-done.21, bf16[16,8,64,128]{3,2,1,0:T(8,128)(2,1)S(1)} %copy-done.3, f32[64,128]{1,0:T(8,128)S(1)} %copy-done.18, f32[64,128]{1,0:T(8,128)S(1)} %copy-done.16, ...), kind=kOutput, calls=%fused_computation.156 | convolution fusion | flops 1619034112 | bytes 31523328 | tf_op jit(solution)/shard_map/nk,rkm->rnm/dot_general | solution.py:101
  680.1 8.6 convolution_bitcast_fusion.3
  696.0 20.5 %fusion.81 = f32[1,128,128,256]{3,2,1,0:T(8,128)} fusion(f32[128,128,128]{1,2,0:T(8,128)} %get-tuple-element.41, f32[128,128,128]{1,2,0:T(8,128)} %get-tuple-element.40, f32[128,128]{1,0:T(8,128)S(1)} %get-tuple-element.86, f32[128,128]{1,0:T(8,128)S(1)} %get-tuple-element.85, f32[128,128]{1,0:T(8,128)S(1)} %fusion.172), kind=kOutput, calls=%fused_computation.89 | convolution fusion | flops 6446841856 | bytes 33751040 | tf_op jit(solution)/shard_map/dot_general | solution.py:80
  716.5 30.8 %multiply_subtract_fusion.1 = (f32[1,128,128,128]{3,2,1,0:T(8,128)}, f32[1,128,128,128]{3,2,1,0:T(8,128)}, f32[1,128,128,128]{3,2,1,0:T(8,128)}, f32[1,128,128,128]{3,2,1,0:T(8,128)}) fusion(f32[1,128,128,256]{3,2,1,0:T(8,128)} %fusion.75, f32[1,128,128,256]{3,2,1,0:T(8,128)} %fusion.81, f32[1,128,128,256]{3,2,1,0:T(8,128)} %fusion.78), kind=kLoop, calls=%fused_computation.104 | loop fusion | flops 27262976 | bytes 83886080 | tf_op jit(solution)/shard_map/sub | solution.py:125
  747.3 14.1 %fusion.65 = f32[128,128,256]{1,2,0:T(8,128)} fusion(f32[1,128,128,128]{3,2,1,0:T(8,128)} %get-tuple-element.17, f32[1,128,128,128]{3,2,1,0:T(8,128)} %get-tuple-element.16, f32[128,128]{1,0:T(8,128)S(1)} %get-tuple-element.86, f32[128,128]{1,0:T(8,128)S(1)} %fusion.172, f32[128,128]{1,0:T(8,128)S(1)} %get-tuple-element.85), kind=kOutput, calls=%fused_computation.77 | convolution fusion | flops 6446841856 | bytes 33751040 | tf_op jit(solution)/shard_map/dot_general | solution.py:88
  761.4 12.9 %fusion.29 = f32[128,128,256]{1,2,0:T(8,128)} fusion(f32[1,128,128,128]{3,2,1,0:T(8,128)S(1)} %copy-done.1, f32[1,128,128,128]{3,2,1,0:T(8,128)} %get-tuple-element.53, f32[128,128]{1,0:T(8,128)S(1)} %get-tuple-element.86, f32[128,128]{1,0:T(8,128)S(1)} %fusion.172, f32[128,128]{1,0:T(8,128)S(1)} %get-tuple-element.85), kind=kOutput, calls=%fused_computation.37 | convolution fusion | flops 6446841856 | bytes 33751040 | tf_op jit(solution)/shard_map/dot_general | solution.py:88
  774.3 22.5 %multiply_add_fusion = (f32[128,128,128]{1,2,0:T(8,128)}, f32[128,128,128]{1,2,0:T(8,128)}, f32[128,128,128]{1,2,0:T(8,128)S(1)}, f32[128,128,128]{1,2,0:T(8,128)}) fusion(f32[128,128,256]{1,2,0:T(8,128)} %fusion.65, f32[128,128]{0,1:T(8,128)S(1)} %copy.241, f32[128,128]{0,1:T(8,128)S(1)} %copy.240, f32[128,128,256]{1,2,0:T(8,128)} %fusion.29), kind=kLoop, calls=%fused_computation.102 | loop fusion | flops 25165824 | bytes 67239936 | tf_op jit(solution)/shard_map/add | solution.py:96
  796.8 11.4 %fusion.116 = f32[128,64,128]{2,1,0:T(8,128)} fusion(f32[128,128,128]{1,2,0:T(8,128)S(1)} %get-tuple-element.68, f32[128,128,128]{1,2,0:T(8,128)} %get-tuple-element.69, f32[64,128]{1,0:T(8,128)S(1)} %copy-done.18, f32[64,128]{1,0:T(8,128)S(1)} %copy-done.16), kind=kOutput, calls=%fused_computation.169 | convolution fusion | flops 1614839808 | bytes 21037056 | tf_op jit(solution)/shard_map/nk,rkm->rnm/dot_general | solution.py:101
  813.3 12.6 %fusion.101 = (bf16[1,1,128,8192]{3,2,1,0:T(8,128)(2,1)}, bf16[1,1,128,8192]{3,2,1,0:T(8,128)(2,1)}, bf16[1,1,128,8192]{3,2,1,0:T(8,128)(2,1)}, bf16[1,1,128,8192]{3,2,1,0:T(8,128)(2,1)S(1)}) fusion(f32[1,1,128,8192]{3,2,1,0:T(8,128)} %reshape_reshape.14, f32[1,1,128,8192]{3,2,1,0:T(8,128)} %reshape_reshape.13, bf16[1,1,128,8192]{3,2,1,0:T(8,128)(2,1)S(1)} %copy-done.5, ...), kind=kLoop, calls=%fused_computation.154 | loop fusion | flops 20971520 | bytes 35652608 | tf_op jit(solution)/shard_map/convert_element_type | solution.py:209
  828.3 29.4 %all_to_all.40 = bf16[8,1,1,1024,128]{3,4,2,1,0:T(8,128)(2,1)S(1)} all-to-all(bf16[8,1,1,1024,128]{3,4,2,1,0:T(8,128)(2,1)S(1)} %fusion.137), channel_id=1, replica_groups=mesh['seq'=8,'tp'=4] {'seq'}, dimensions={0} | all-to-all | bytes 4194304 | tf_op jit(solution)/shard_map/all_to_all | solution.py:15
  857.6 14.6 %convert_bitcast_fusion = bf16[4096,1024]{0,1:T(8,128)(2,1)} fusion(bf16[1024,1024]{0,1:T(8,128)(2,1)S(1)} %bitcast.286, bf16[1024,4096]{1,0:T(8,128)(2,1)} %param.10), kind=kOutput, calls=%fused_computation.121 | convolution fusion | flops 8594128896 | bytes 18874368 | tf_op jit(solution)/shard_map/dot_general | solution.py:178
  891.1 12.6 %fusion.107 = f32[128,64,128]{2,1,0:T(8,128)} fusion(f32[128,128,128]{1,2,0:T(8,128)} %get-tuple-element.27, f32[128,128,128]{1,2,0:T(8,128)} %get-tuple-element.26, f32[64,128]{1,0:T(8,128)S(1)} %copy-done.18, f32[64,128]{1,0:T(8,128)S(1)} %copy-done.16), kind=kOutput, calls=%fused_computation.166 | convolution fusion | flops 1614839808 | bytes 21037056 | tf_op jit(solution)/shard_map/nk,rkm->rnm/dot_general | solution.py:101
  908.7 12.7 %fusion.104 = f32[128,64,128]{2,1,0:T(8,128)} fusion(f32[128,128,128]{1,2,0:T(8,128)} %get-tuple-element.29, f32[128,128,128]{1,2,0:T(8,128)} %get-tuple-element.28, f32[64,128]{1,0:T(8,128)S(1)} %copy-done.18, f32[64,128]{1,0:T(8,128)S(1)} %copy-done.16), kind=kOutput, calls=%fused_computation.165 | convolution fusion | flops 1614839808 | bytes 21037056 | tf_op jit(solution)/shard_map/nk,rkm->rnm/dot_general | solution.py:101
  926.5 32.7 %all-to-all-done.3 = bf16[8,3,1,1024,128]{3,4,1,2,0:T(8,128)(2,1)} async-done(((bf16[8,3,1,1024,128]{3,4,1,2,0:T(8,128)(2,1)}), bf16[8,3,1,1024,128]{3,4,1,2,0:T(8,128)(2,1)}, u32[]{:S(2)}, u32[]{:S(2)}) %all-to-all-start.3) | async-done | bytes 6291488 | tf_op jit(solution)/shard_map/all_to_all | solution.py:15
  959.2 11.5 %copy.274 = bf16[3,1,1024,8,128]{2,0,4,3,1:T(4,128)(2,1)} copy(bf16[3,1,1024,8,128]{2,4,0,1,3:T(8,128)(2,1)} %bitcast.75) | data formatting | bytes 12582912 | tf_op jit(solution)/shard_map/reshape | solution.py:16
  987.3 10.3 maximum_convert_fusion.1
  997.6 33.0 %fusion.1 = bf16[1,1024,3,1024]{1,2,0,3:T(4,128)(2,1)} fusion(f32[1,1026,3,1024]{1,2,0,3:T(4,128)} %maximum_convert_fusion.1, f32[3,1024]{0,1:T(8,128)S(1)} %bitcast.283, f32[3,1024]{0,1:T(8,128)S(1)} %bitcast.285, f32[3,1024]{0,1:T(8,128)S(1)} %bitcast.281), kind=kLoop, calls=%fused_computation.2 | loop fusion | flops 18874368 | bytes 44077056 | tf_op jit(solution)/shard_map/convert_element_type | solution.py:220
  1030.6 13.0 %copy.283 = bf16[1,1024,3,1024]{3,1,2,0:T(8,128)(2,1)} copy(bf16[1,1024,3,1024]{1,2,0,3:T(4,128)(2,1)} %fusion.1) | data formatting | bytes 12582912
  (126 shorter events, 159.3 us)
Async XLA Ops:
  7.2 154.3 %all-gather.2.cloned.1.call-start = ((), (), s32[]{:S(2)}) async-start(), calls=%async_computation.6 | async-start | bytes 10485760 | tf_op jit(solution)/shard_map/all_gather | solution.py:187
  8.7 20.8 %collective-permute-start = (bf16[1,2,3,1024]{3,1,2,0:T(2,128)(2,1)S(1)}, bf16[1,2,3,1024]{3,1,2,0:T(2,128)(2,1)S(1)}, u32[]{:S(2)}, u32[]{:S(2)}) collective-permute-start(bf16[1,2,3,1024]{3,1,2,0:T(2,128)(2,1)S(1)} %slice.194), channel_id=1, source_target_pairs={{0,4},{4,8},{8,12},{12,16},{16,20},{20,24},{24,28},{1,5},{5,9},{9,... | collective-permute-start | bytes 36872 | tf_op jit(solution)/shard_map/ppermute | solution.py:22
  29.0 12.1 %copy-start.7 = (f32[3,1,1024]{0,2,1:T(8,128)}, f32[3,1,1024]{0,2,1:T(8,128)S(1)}, u32[]{:S(2)}) copy-start(f32[3,1,1024]{0,2,1:T(8,128)S(1)} %copy.308) | copy-start | bytes 36868
  29.3 11.9 %copy-start.9 = (f32[3,1,1024]{0,2,1:T(8,128)}, f32[3,1,1024]{0,2,1:T(8,128)S(1)}, u32[]{:S(2)}) copy-start(f32[3,1,1024]{0,2,1:T(8,128)S(1)} %copy.310) | copy-start | bytes 36868
  29.5 11.7 %copy-start.11 = (f32[3,1,1024]{0,2,1:T(8,128)}, f32[3,1,1024]{0,2,1:T(8,128)S(1)}, u32[]{:S(2)}) copy-start(f32[3,1,1024]{0,2,1:T(8,128)S(1)} %copy.309) | copy-start | bytes 36868
  71.0 129.0 %all-to-all-start = ((bf16[3,1,1024,1024]{2,0,1,3:T(4,128)(2,1)}), bf16[3,1,1024,1024]{2,0,1,3:T(4,128)(2,1)}, u32[]{:S(2)}, u32[]{:S(2)}) async-start(bf16[3,1,1024,1024]{2,0,1,3:T(4,128)(2,1)} %fusion.92), calls=%async_computation | async-start | bytes 16777216 | tf_op jit(solution)/shard_map/all_to_all | solution.py:137
  81.8 3.8 copy-start.22
  86.7 329.0 %copy-start.13 = (f32[128,64]{1,0:T(8,128)}, f32[128,64]{1,0:T(8,128)S(1)}, u32[]{:S(2)}) copy-start(f32[128,64]{1,0:T(8,128)S(1)} %slice_negate_fusion) | copy-start | bytes 98308
  200.0 51.7 %all-to-all-start.2 = ((bf16[8,2,65536]{2,1,0:T(2,128)(2,1)}), bf16[8,2,65536]{2,1,0:T(2,128)(2,1)S(1)}, u32[]{:S(2)}, u32[]{:S(2)}) async-start(bf16[8,2,65536]{2,1,0:T(2,128)(2,1)} %reshape.366), calls=%async_computation.3 | async-start | bytes 4194304 | tf_op jit(solution)/shard_map/all_to_all | solution.py:137
  204.1 839.5 %reduce-scatter.2.cloned.1.call-start = ((), (), s32[]{:S(2)}) async-start(), calls=%async_computation.5 | async-start | bytes 10485760 | tf_op jit(solution)/shard_map/reduce_scatter | solution.py:177
  240.4 2.8 copy-start.2
  279.3 1.3 copy-start.4
  388.8 9.6 copy-start
  388.8 9.6 copy-start.15
  388.8 9.6 copy-start.17
  388.8 9.6 copy-start.19
  570.5 27.9 %slice-start = ((s8[8388608]{0:T(1024)(128)(4,1)}), s8[4194304]{0:T(1024)(128)(4,1)S(1)}, s32[]{:S(2)}) async-start(s8[8388608]{0:T(1024)(128)(4,1)} %bitcast.265), calls=%async_computation.7 | async-start | bytes 8388608
  584.5 13.8 %slice-start.1 = ((s8[8388608]{0:T(1024)(128)(4,1)}), s8[4194304]{0:T(1024)(128)(4,1)S(1)}, s32[]{:S(2)}) async-start(s8[8388608]{0:T(1024)(128)(4,1)} %bitcast.265), calls=%async_computation.8 | async-start | bytes 8388608
  611.4 31.7 %copy-start.16 = (f32[64,128]{1,0:T(8,128)S(1)}, f32[64,128]{1,0:T(8,128)}, u32[]{:S(2)}) copy-start(f32[64,128]{1,0:T(8,128)} %slice.271) | copy-start | bytes 98308
  611.4 31.7 %copy-start.18 = (f32[64,128]{1,0:T(8,128)S(1)}, f32[64,128]{1,0:T(8,128)}, u32[]{:S(2)}) copy-start(f32[64,128]{1,0:T(8,128)} %slice_negate_fusion.1) | copy-start | bytes 98308
  656.1 5.1 copy-start.3
  656.1 5.1 copy-start.21
  675.2 5.0 copy-start.14
  747.3 14.1 %copy-start.1 = (f32[1,128,128,128]{3,2,1,0:T(8,128)S(1)}, f32[1,128,128,128]{3,2,1,0:T(8,128)}, u32[]{:S(2)}) copy-start(f32[1,128,128,128]{3,2,1,0:T(8,128)} %get-tuple-element.52) | copy-start | bytes 25165828
  808.2 5.1 copy-start.5
  808.2 5.1 copy-start.20
  872.3 1.6 copy-start.6
  885.1 74.1 %all-to-all-start.3 = ((bf16[8,3,1,1024,128]{3,4,1,2,0:T(8,128)(2,1)}), bf16[8,3,1,1024,128]{3,4,1,2,0:T(8,128)(2,1)}, u32[]{:S(2)}, u32[]{:S(2)}) async-start(bf16[8,3,1,1024,128]{3,4,1,2,0:T(8,128)(2,1)} %fusion.125), calls=%async_computation.4 | async-start | bytes 12582912 | tf_op jit(solution)/shard_map/all_to_all | solution.py:15
  972.9 13.6 %collective-permute-start.1 = (bf16[1,2,3,1024]{3,1,2,0:T(2,128)(2,1)S(1)}, bf16[1,2,3,1024]{3,1,2,0:T(2,128)(2,1)S(1)}, u32[]{:S(2)}, u32[]{:S(2)}) collective-permute-start(bf16[1,2,3,1024]{3,1,2,0:T(2,128)(2,1)S(1)} %copy.275), channel_id=1, source_target_pairs={{4,0},{8,4},{12,8},{16,12},{20,16},{24,20},{28,24},{5,1},{9,5},{13... | collective-permute-start | bytes 36872 | tf_op jit(solution)/shard_map/ppermute | solution.py:22
  987.2 10.3 copy-start.8
  987.3 10.3 copy-start.10
  987.3 10.3 copy-start.12
Sparse Core Ops, SparseCore 0:
  9.5 151.8 all-gather.1
  872.4 141.1 reduce-scatter.1
